TPU v7x, 32 devices: a whole 2x2x4 slice. The times are simulated.
32 devices in a mesh: parts: 2 (over y), tensor: 4 (over z), dp: 4 (over x, core).
Axes of the slice: x: 2, y: 2, z: 4, core: 2. Of those that a mesh axis runs over, the one named last changes fastest.
Arguments:
- inputs: bfloat16 [4096, 8192], P(('parts', 'dp'), 'tensor'), parts along dimension 0, may hold values from -6 to 6
- cotangent: bfloat16 [4096, 8192], P(('parts', 'dp'), 'tensor'), parts along dimension 0, may hold values from -6 to 6
- weight: bfloat16 [8192, 8192], P(None, 'tensor'), may hold values from -0.0625 to 0.0625
- down_weight_maps: bfloat16 [8192, 2048], P('tensor', 'parts'), parts along dimension 1, may hold values from -0.0625 to 0.0625
- up_weight_maps: bfloat16 [2048, 8192], P('parts', 'tensor'), parts along dimension 0, may hold values from -0.75 to 0.75
- counts: int32 [8, 16], P('parts'), parts along dimension 0, may hold values from 0 to 256, as said below
- ranks: int32 [32], P('parts'), parts along dimension 0, may hold values from 8 to 64, as said below
- owners: int32 [32], P('parts'), parts along dimension 0, may hold values from 0 to 3
Outputs:
- projected: bfloat16 [4096, 8192], P(('parts', 'dp'), 'tensor'), parts along dimension 0
- input_grad: bfloat16 [4096, 8192], P(('parts', 'dp'), 'tensor'), parts along dimension 0
- grad_a: float32 [8, 8192, 1024], P(('parts', 'dp'), 'tensor'), parts along dimension 0
- grad_b: float32 [8, 1024, 8192], P(('parts', 'dp'), None, 'tensor'), parts along dimension 0
There are 2 independent parts, one for each index of `parts`. A program takes and returns all parts, laid end to end along the dimension named above; an argument that names none is the same for every part. Nothing has to cross between parts.
Inputs may be any that keep to these rules, and one draw needn't show every extreme that they name: `counts`: each row sums to at most 512, one row to exactly 512, and all rows together to exactly 1024; some entry is exactly 256. `ranks`: each rank is 64 divided by 1, 2, 4 or 8; some trial has 64 and some 64 // 8.
All inputs are finite; a program needn't handle non-finite values.
Results may differ from a plain program's by a relative error of at most 0.0034.
Values may be sent and summed in bfloat16 or wider, within the bound.
A program may use at most 256 MiB of HBM per device.

v0:
```python
import jax
import jax.numpy as jnp
from jax import lax
from jax.sharding import PartitionSpec as P

LARGEST_RANK = 64
TRIALS = 16
adapter_alpha = 16.0


def local(inputs, cotangent, weight, down_weight_maps, up_weight_maps, counts, ranks, owners):
    slot_count, feature_local = inputs.shape
    group_count = counts.shape[0]
    adapter_rank_width = down_weight_maps.shape[1]
    column = jnp.arange(adapter_rank_width, dtype=jnp.int32)
    col_trial = column // LARGEST_RANK
    column_slot = column % LARGEST_RANK
    trial_ids = jnp.arange(TRIALS, dtype=jnp.int32)
    matches = col_trial[:, None] == trial_ids[None, :]
    rank_per_column = jnp.sum(jnp.where(matches, ranks[None, :], 0), axis=1)
    owner_col = jnp.sum(jnp.where(matches, owners[None, :], 0), axis=1)
    scale_per_column = jnp.where(
        column_slot < rank_per_column, adapter_alpha / rank_per_column.astype(jnp.float32), 0.0
    )
    trial_rows = jnp.sum(counts, axis=0)
    per_trial = 1.0 / jnp.maximum(trial_rows, 1).astype(jnp.float32)
    inverse_col = jnp.sum(jnp.where(matches, per_trial[None, :], 0.0), axis=1)
    cumulative = jnp.cumsum(counts, axis=1)
    group_ids = jnp.arange(group_count, dtype=jnp.int32)
    my_group = lax.axis_index("dp")
    contract_trailing = (((1,), (1,)), ((), ()))
    contract_first = (((0,), (0,)), ((), ()))
    positions = jnp.arange(slot_count, dtype=jnp.int32)
    my_bounds = jnp.sum(jnp.where((group_ids == my_group)[:, None], cumulative, 0), axis=0)
    row_trial = jnp.sum((positions[:, None] >= my_bounds[None, :]).astype(jnp.int32), axis=1)
    is_live = row_trial < TRIALS
    coef = jnp.where(row_trial[:, None] == col_trial[None, :], scale_per_column[None, :], 0.0)
    frozen_output = jnp.dot(
        lax.all_gather(inputs, "tensor", axis=1, tiled=True),
        weight,
        preferred_element_type=jnp.float32,
    )
    down_projected_sum = lax.psum(
        jnp.dot(inputs, down_weight_maps, preferred_element_type=jnp.float32), "tensor"
    )
    scaled_down_projected = (coef * down_projected_sum).astype(jnp.bfloat16)
    merged_output = frozen_output + jnp.dot(
        scaled_down_projected, up_weight_maps, preferred_element_type=jnp.float32
    )
    result = jnp.where(is_live[:, None], merged_output, 0.0).astype(jnp.bfloat16)
    back_part = lax.dot_general(
        cotangent, up_weight_maps, contract_trailing, preferred_element_type=jnp.float32
    )
    back_sum = lax.psum(back_part, "tensor")
    scaled_up_projected = (coef * back_sum).astype(jnp.bfloat16)
    frozen_back = lax.dot_general(
        cotangent, weight, contract_trailing, preferred_element_type=jnp.float32
    )
    frozen_share = lax.psum_scatter(frozen_back, "tensor", scatter_dimension=1, tiled=True)
    adapter_in = lax.dot_general(
        scaled_up_projected, down_weight_maps, contract_trailing, preferred_element_type=jnp.float32
    )
    gradient = jnp.where(is_live[:, None], frozen_share + adapter_in, 0.0).astype(jnp.bfloat16)
    term_a = (
        lax.dot_general(
            inputs, scaled_up_projected, contract_first, preferred_element_type=jnp.float32
        )
        * inverse_col[None, :]
    )
    term_b = (
        lax.dot_general(
            scaled_down_projected, cotangent, contract_first, preferred_element_type=jnp.float32
        )
        * inverse_col[:, None]
    )
    projected, input_grad, term_a, term_b = (result, gradient, term_a, term_b)
    full_a, full_b = lax.psum((term_a, term_b), "dp")
    owned_mine = (owner_col == my_group).astype(jnp.float32)
    grad_a = (full_a * owned_mine[None, :])[None]
    grad_b = (full_b * owned_mine[:, None])[None]
    return (projected, input_grad, grad_a, grad_b)


def solution(mesh):
    return jax.shard_map(
        local,
        mesh=mesh,
        in_specs=(
            P(("parts", "dp"), "tensor"),
            P(("parts", "dp"), "tensor"),
            P(None, "tensor"),
            P("tensor", "parts"),
            P("parts", "tensor"),
            P("parts", None),
            P("parts"),
            P("parts"),
        ),
        out_specs=(
            P(("parts", "dp"), "tensor"),
            P(("parts", "dp"), "tensor"),
            P(("parts", "dp"), "tensor", None),
            P(("parts", "dp"), None, "tensor"),
        ),
        check_vma=False,
    )
```

profile of v0, /device:TPU:0, one launch (start us, length us, event | category | flops | bytes accessed | tf_op | source)
XLA Modules:
  0.0 924.6 jit_solution(6488323135650758244)
XLA Ops:
  7.2 0.0 copy-start
  7.2 0.0 all-reduce.7.cloned.1.call-start
  7.2 0.0 copy-start.7
  7.2 6.6 fusion.15
  13.9 3.7 fusion.17
  17.6 0.0 all-reduce.7.cloned.1.call-update
  17.6 0.0 all-reduce.5.cloned.1.call-start
  17.6 0.6 copy-done.4
  18.2 0.2 reduce_window_sum.11
  18.5 0.1 select_reduce_fusion.3
  18.5 0.1 convert_reduce_fusion
  18.6 0.1 select_reduce_fusion.1
  18.8 0.1 select_reduce_fusion
  18.9 156.9 %all-reduce.7.cloned.1.call-done = (f32[512,1024]{1,0:T(8,128)}, f32[512,1024]{1,0:T(8,128)}) async-done(((f32[512,1024]{1,0:T(8,128)}, f32[512,1024]{1,0:T(8,128)}), (f32[512,1024]{1,0:T(8,128)}, f32[512,1024]{1,0:T(8,128)})) %all-reduce.7.cloned.1.call-update) | async-done | bytes 4194320 | tf_op jit(solution)/shard_map/psum | solution.py:43
  175.8 8.2 multiply_bitcast_fusion.2
  184.0 5.9 convolution_multiply_fusion
  189.9 0.0 all-reduce.5.cloned.1.call-update
  190.0 0.0 all-gather.2.cloned.1.call-start
  190.0 0.7 all-gather.2.cloned.1.call-update
  190.7 0.2 reduce-scatter.2.cloned.1.call-start
  190.9 25.8 %fusion.16 = f32[512,8192]{1,0:T(8,128)} fusion(bf16[512,2048]{1,0:T(8,128)(2,1)S(1)} %copy-done, bf16[8192,2048]{1,0:T(8,128)(2,1)} %param.10), kind=kOutput, calls=%fused_computation.36 | convolution fusion | flops 17179869184 | bytes 52428800 | tf_op jit(solution)/shard_map/dot_general | solution.py:56
  216.7 0.0 reduce-scatter.2.cloned.1.call-update
  216.8 1.6 copy-done.3
  218.4 6.5 fusion.13
  224.9 253.1 %all-reduce.5.cloned.1.call-done = (f32[2048,1024]{0,1:T(8,128)}, f32[1024,2048]{1,0:T(8,128)}) async-done(((f32[2048,1024]{0,1:T(8,128)}, f32[1024,2048]{1,0:T(8,128)}), (f32[2048,1024]{0,1:T(8,128)}, f32[1024,2048]{1,0:T(8,128)})) %all-reduce.5.cloned.1.call-update) | async-done | bytes 16777232 | tf_op jit(solution)/shard_map/psum | solution.py:77
  478.0 7.4 multiply_bitcast_fusion.1
  485.3 9.7 %copy.13 = f32[1,2048,1024]{2,1,0:T(8,128)} copy(f32[1,2048,1024]{1,2,0:T(8,128)} %multiply_bitcast_fusion.1) | data formatting | bytes 16777216
  495.1 7.4 multiply_bitcast_fusion
  502.5 126.8 %all-gather.2.cloned.1.call-done = bf16[512,8192]{1,0:T(8,128)(2,1)} async-done(((bf16[512,2048]{1,0:T(8,128)(2,1)}), bf16[512,8192]{1,0:T(8,128)(2,1)}) %all-gather.2.cloned.1.call-update) | async-done | bytes 8388624 | tf_op jit(solution)/shard_map/all_gather | solution.py:39
  629.3 24.9 %select_convert_fusion.1 = bf16[512,2048]{1,0:T(8,128)(2,1)} fusion(f32[512,2048]{1,0:T(8,128)} %fusion.13, bf16[512,8192]{1,0:T(8,128)(2,1)} %all-gather.2.cloned.1.call-done, bf16[8192,2048]{1,0:T(8,128)(2,1)} %param.10, pred[512]{0:T(512)(128)(4,1)S(1)} %broadcast_compare_fusion), kind=kOutput, calls=%fused_computation.5 | convolution fusion | flops 17183014912 | bytes 48235008 | tf_op jit(solution)/shard_map/dot_general | solution.py:38
  654.2 255.9 %reduce-scatter.2.cloned.1.call-done = f32[512,2048]{1,0:T(8,128)} async-done(((f32[512,8192]{1,0:T(8,128)}), f32[512,2048]{1,0:T(8,128)}) %reduce-scatter.2.cloned.1.call-update) | async-done | bytes 4194320 | tf_op jit(solution)/shard_map/reduce_scatter | solution.py:59
  910.1 7.9 select_convert_fusion
  (19 shorter events, 0.1 us)
Async XLA Ops:
  7.2 6.7 copy-start
  7.2 168.6 %all-reduce.7.cloned.1.call-start = ((), (), s32[]{:S(2)}) async-start(), calls=%async_computation.4 | async-start | bytes 8388608 | tf_op jit(solution)/shard_map/psum | solution.py:43
  7.2 6.6 copy-start.7
  17.5 0.7 copy-start.4
  17.6 1.2 copy-start.5
  17.6 1.2 copy-start.6
  17.6 460.4 %all-reduce.5.cloned.1.call-start = ((), (), s32[]{:S(2)}) async-start(), calls=%async_computation.3 | async-start | bytes 33554432 | tf_op jit(solution)/shard_map/psum | solution.py:77
  175.8 8.3 copy-start.2
  190.0 439.3 %all-gather.2.cloned.1.call-start = ((), (), s32[]{:S(2)}) async-start(), calls=%async_computation.1 | async-start | bytes 10485760 | tf_op jit(solution)/shard_map/all_gather | solution.py:39
  190.7 719.4 %reduce-scatter.2.cloned.1.call-start = ((), (), s32[]{:S(2)}) async-start(), calls=%async_computation.2 | async-start | bytes 20971520 | tf_op jit(solution)/shard_map/reduce_scatter | solution.py:59
  216.7 1.7 copy-start.3
  910.1 7.9 copy-start.1
Sparse Core Ops, SparseCore 0:
  17.7 158.0 all-reduce.6
  190.1 287.8 all-reduce.4
  479.6 149.6 all-gather.1
  631.6 278.4 reduce-scatter.1
where the time goes:
time: 925 us
  waiting for transfers between devices  793 us (86%)
  matrix products  89.6 us (10%)
  other arithmetic  15.4 us (2%)
  between operations  13.9 us (2%)
  local copies, waits for them, and re-layouts  12 us (1%)
    reduce_scatter x1, waiting for transfers between devices, local(): lax.psum_scatter(frozen_back, 'tensor', scatter_dimension=1, tiled=True)  256 us
    psum x1, waiting for transfers between devices, local(): full_a, full_b = lax.psum((term_a, term_b), 'dp')  253 us
    psum x1, waiting for transfers between devices, local(): lax.psum(jnp.dot(inputs, down_weight_maps, preferred_element_type=jnp.flo...  157 us
    all_gather x1, waiting for transfers between devices, local(): lax.all_gather(inputs, 'tensor', axis=1, tiled=True)  127 us
    dot_general x1, matrix products, local(): lax.dot_general(cotangent, weight, contract_trailing, preferred_element_t...  25.8 us
    dot_general x1, matrix products, local(): jnp.dot(lax.all_gather(inputs, 'tensor', axis=1, tiled=True), weight, pre...  24.9 us
  transfers between devices with their start and end apart: 4, of which 4 were waited for; matrix products, arithmetic and copies ran while one was open for 9% of the time, Pallas kernels for 0%

commit v1 on v0

--- a/solution.py
+++ b/solution.py
@@ -6,6 +6,33 @@
 LARGEST_RANK = 64
 TRIALS = 16
 adapter_alpha = 16.0
+
+
+def point_the_page(point, ndim_at):
+    point = jnp.moveaxis(point, 0, ndim_at)
+    seen_now = point.shape
+    return point.reshape(
+        *seen_now[:ndim_at], seen_now[ndim_at] * seen_now[ndim_at + 1], *seen_now[ndim_at + 2 :]
+    )
+
+
+def digits_manage(u, shard_axis):
+    ndev = lax.axis_size(shard_axis)
+    part_now = u[None]
+    for nth in range(ndev.bit_length() - 1):
+        piece_now = 1 << nth
+        kept_arr = lax.ppermute(
+            part_now, axis_name=shard_axis, perm=[(k0, k0 ^ piece_now) for k0 in range(ndev)]
+        )
+        t1 = jnp.stack([part_now, kept_arr], axis=0)
+        m_next = lax.axis_index(shard_axis) >> nth & 1
+        part_now = jnp.where(m_next == 0, t1, t1[::-1]).reshape(-1, *u.shape)
+    return part_now
+
+
+def serve_cubes_here(z_in, xs, dim_no):
+    x_now = digits_manage(z_in, xs)
+    return point_the_page(x_now, dim_no)
 
 
 def local(inputs, cotangent, weight, down_weight_maps, up_weight_maps, counts, ranks, owners):
@@ -36,9 +63,7 @@
     is_live = row_trial < TRIALS
     coef = jnp.where(row_trial[:, None] == col_trial[None, :], scale_per_column[None, :], 0.0)
     frozen_output = jnp.dot(
-        lax.all_gather(inputs, "tensor", axis=1, tiled=True),
-        weight,
-        preferred_element_type=jnp.float32,
+        serve_cubes_here(inputs, "tensor", 1), weight, preferred_element_type=jnp.float32
     )
     down_projected_sum = lax.psum(
         jnp.dot(inputs, down_weight_maps, preferred_element_type=jnp.float32), "tensor"

time: 925 us -> 776 us (0.84)
  waiting for transfers between devices: 793 us -> 604 us
  other arithmetic: 15.4 us -> 43 us
  local copies, waits for them, and re-layouts: 12 us -> 22.8 us
    psum x1, waiting for transfers between devices: 253 us -> 0.01 us  [local(): full_a, full_b = lax.psum((term_a, term_b), 'dp')]
    ppermute x0 -> x2, waiting for transfers between devices: none -> 222 us  [digits_manage(): lax.ppermute(part_now, axis_name=shard_axis, perm=[(k0, k0 ^ piece_now) f...]
    all_gather x1 -> x0, waiting for transfers between devices: 127 us -> none  [local(): lax.all_gather(inputs, 'tensor', axis=1, tiled=True)]
    reduce_scatter x1, waiting for transfers between devices: 256 us -> 225 us  [local(): lax.psum_scatter(frozen_back, 'tensor', scatter_dimension=1, tiled=True)]
    select_n x0 -> x1, other arithmetic: none -> 14.4 us  [digits_manage(): part_now = jnp.where(m_next == 0, t1, t1[::-1]).reshape(-1, *u.shape)]
    another operation x0 -> x3, other arithmetic: none -> 13.3 us  [digits_manage(): t1 = jnp.stack([part_now, kept_arr], axis=0)]
    select_n x0 -> x1, local copies, waits for them, and re-layouts: none -> 11.4 us  [digits_manage(): part_now = jnp.where(m_next == 0, t1, t1[::-1]).reshape(-1, *u.shape)]
  transfers between devices with their start and end apart: 4 -> 5, of which waited for: 4 -> 4; matrix products, arithmetic and copies ran while one was open for 9% -> 16% of each run, Pallas kernels for 0% -> 0%
where the time goes in v1:
time: 776 us; the launch traced here: 775 us
  waiting for transfers between devices  604 us (78%)
  matrix products  89.4 us (12%)
  other arithmetic  43 us (6%)
  local copies, waits for them, and re-layouts  22.8 us (3%)
  between operations  13.9 us (2%)
    reduce_scatter x1, waiting for transfers between devices, local(): lax.psum_scatter(frozen_back, 'tensor', scatter_dimension=1, tiled=True)  225 us
    ppermute x2, waiting for transfers between devices, digits_manage(): lax.ppermute(part_now, axis_name=shard_axis, perm=[(k0, k0 ^ piece_now) f...  222 us
    psum x1, waiting for transfers between devices, local(): lax.psum(jnp.dot(inputs, down_weight_maps, preferred_element_type=jnp.flo...  157 us
    dot_general x1, matrix products, local(): jnp.dot(serve_cubes_here(inputs, 'tensor', 1), weight, preferred_element_...  25.6 us
    dot_general x1, matrix products, local(): lax.dot_general(cotangent, weight, contract_trailing, preferred_element_t...  25.1 us
  transfers between devices with their start and end apart: 5, of which 4 were waited for; matrix products, arithmetic and copies ran while one was open for 16% of the time, Pallas kernels for 0%

profile of v1, /device:TPU:0, one launch (start us, length us, event | category | flops | bytes accessed | tf_op | source)
XLA Modules:
  0.0 774.9 jit_solution(3674183715210247501)
XLA Ops:
  7.2 0.0 all-reduce.7.cloned.1.call-start
  7.2 6.6 fusion.17
  13.9 3.7 fusion.19
  17.6 0.0 all-reduce.7.cloned.1.call-update
  17.6 0.0 all-reduce.5.cloned.1.call-start
  17.6 0.6 copy-done.6
  18.2 0.2 reduce_window_sum.11
  18.5 0.1 select_reduce_fusion.3
  18.5 0.1 convert_reduce_fusion
  18.6 0.1 select_reduce_fusion.1
  18.8 0.1 select_reduce_fusion
  18.9 156.9 %all-reduce.7.cloned.1.call-done = (f32[512,1024]{1,0:T(8,128)}, f32[512,1024]{1,0:T(8,128)}) async-done(((f32[512,1024]{1,0:T(8,128)}, f32[512,1024]{1,0:T(8,128)}), (f32[512,1024]{1,0:T(8,128)}, f32[512,1024]{1,0:T(8,128)})) %all-reduce.7.cloned.1.call-update) | async-done | bytes 4194320 | tf_op jit(solution)/shard_map/psum | solution.py:68
  175.8 8.1 %multiply_bitcast_fusion.2 = f32[2048,1024]{0,1:T(8,128)} fusion(bf16[512,2048]{1,0:T(8,128)(2,1)} %param.8, f32[1024]{0:T(1024)S(1)} %select_reduce_fusion.1, f32[512,1024]{1,0:T(8,128)} %get-tuple-element.21, f32[1024]{0:T(1024)S(1)} %divide_select_fusion, s32[1024]{0:T(1024)S(1)} %add_select_fusion, s32[512]{0:T(512)S(1)} %convert_reduce_fusion), kind=kOutput, calls=%fused_computation.4 | convolution fusion | flops 2151677952 | bytes 12597248 | tf_op jit(solution)/shard_map/dot_general | solution.py:90
  183.8 5.7 convolution_multiply_fusion
  189.6 0.2 reduce-scatter.2.cloned.1.call-start
  189.8 25.1 %fusion.18 = f32[512,8192]{1,0:T(8,128)} fusion(bf16[512,2048]{1,0:T(8,128)(2,1)S(1)} %copy-done, bf16[8192,2048]{1,0:T(8,128)(2,1)} %param.10), kind=kOutput, calls=%fused_computation.42 | convolution fusion | flops 17179869184 | bytes 52428800 | tf_op jit(solution)/shard_map/dot_general | solution.py:81
  215.0 1.6 copy-done.3
  216.5 47.4 %collective-permute-done = bf16[1,512,2048]{2,1,0:T(8,128)(2,1)} collective-permute-done((bf16[1,512,2048]{2,1,0:T(8,128)(2,1)S(1)}, bf16[1,512,2048]{2,1,0:T(8,128)(2,1)}, u32[]{:S(2)}, u32[]{:S(2)}) %collective-permute-start) | collective-permute-done | bytes 2097184 | tf_op jit(solution)/shard_map/ppermute | solution.py:24
  264.0 2.0 pad_maximum_fusion.1
  265.9 5.0 fusion.1
  270.9 1.4 collective-permute-start.1
  272.4 6.7 fusion.15
  279.0 174.3 %collective-permute-done.1 = bf16[2,512,2048]{2,1,0:T(8,128)(2,1)} collective-permute-done((bf16[2,512,2048]{2,1,0:T(8,128)(2,1)}, bf16[2,512,2048]{2,1,0:T(8,128)(2,1)}, u32[]{:S(2)}, u32[]{:S(2)}) %collective-permute-start.1) | collective-permute-done | bytes 4194336 | tf_op jit(solution)/shard_map/ppermute | solution.py:24
  453.4 6.4 pad_maximum_fusion
  459.7 14.4 %reverse_select_fusion = bf16[2,2,512,2048]{3,2,1,0:T(8,128)(2,1)} fusion(bf16[2,2,512,2048]{3,2,1,0:T(8,128)(2,1)} %pad_maximum_fusion, pred[]{:T(512)S(6)} %eq.72), kind=kLoop, calls=%fused_computation | loop fusion | flops 4194304 | bytes 16777216 | tf_op jit(solution)/shard_map/jit(_where)/select_n | solution.py:29
  474.1 11.4 %copy.15 = bf16[2,2,512,2048]{2,3,1,0:T(8,128)(2,1)} copy(bf16[2,2,512,2048]{3,2,1,0:T(8,128)(2,1)} %reverse_select_fusion) | data formatting | bytes 16777216 | tf_op jit(solution)/shard_map/jit(_where)/select_n | solution.py:29
  485.5 25.6 %select_convert_fusion.1 = bf16[512,2048]{1,0:T(8,128)(2,1)} fusion(f32[512,2048]{1,0:T(8,128)} %fusion.15, bf16[512,8192]{0,1:T(8,128)(2,1)} %bitcast.31, bf16[8192,2048]{1,0:T(8,128)(2,1)} %param.10, pred[512]{0:T(512)(128)(4,1)S(1)} %broadcast_compare_fusion), kind=kOutput, calls=%fused_computation.9 | convolution fusion | flops 17183014912 | bytes 48235008 | tf_op jit(solution)/shard_map/dot_general | solution.py:65
  511.1 7.4 multiply_bitcast_fusion.1
  518.4 9.2 %copy.16 = f32[1,2048,1024]{2,1,0:T(8,128)} copy(f32[1,2048,1024]{1,2,0:T(8,128)} %multiply_bitcast_fusion.1) | data formatting | bytes 16777216
  527.7 7.4 multiply_bitcast_fusion
  535.1 225.3 %reduce-scatter.2.cloned.1.call-done = f32[512,2048]{1,0:T(8,128)} async-done(((f32[512,8192]{1,0:T(8,128)}), f32[512,2048]{1,0:T(8,128)}) %reduce-scatter.2.cloned.1.call-update) | async-done | bytes 4194320 | tf_op jit(solution)/shard_map/reduce_scatter | solution.py:84
  760.4 7.9 %select_convert_fusion = bf16[512,2048]{1,0:T(8,128)(2,1)} fusion(f32[512,2048]{1,0:T(8,128)} %reduce-scatter.2.cloned.1.call-done, bf16[2048,1024]{1,0:T(8,128)(2,1)} %param.11, pred[512]{0:T(512)(128)(4,1)S(1)} %broadcast_compare_fusion, f32[512,1024]{1,0:T(8,128)} %get-tuple-element.21, f32[1024]{0:T(1024)S(1)} %divide_select_fusion, ...), kind=kOutput, calls=%fused_computation.8 | convolution fusion | flops 2152726528 | bytes 12593664 | tf_op jit(solution)/shard_map/dot_general | solution.py:85
  (29 shorter events, 0.1 us)
Async XLA Ops:
  7.2 6.7 copy-start
  7.2 168.6 %all-reduce.7.cloned.1.call-start = ((), (), s32[]{:S(2)}) async-start(), calls=%async_computation.3 | async-start | bytes 8388608 | tf_op jit(solution)/shard_map/psum | solution.py:68
  7.2 6.6 copy-start.9
  17.5 0.7 copy-start.6
  17.6 1.2 copy-start.7
  17.6 1.2 copy-start.8
  17.6 493.5 %all-reduce.5.cloned.1.call-start = ((), (), s32[]{:S(2)}) async-start(), calls=%async_computation.2 | async-start | bytes 33554432 | tf_op jit(solution)/shard_map/psum | solution.py:102
  175.8 8.1 %copy-start.4 = (f32[512,1024]{1,0:T(8,128)S(1)}, f32[512,1024]{1,0:T(8,128)}, u32[]{:S(2)}) copy-start(f32[512,1024]{1,0:T(8,128)} %get-tuple-element.20) | copy-start | bytes 6291460
  189.6 570.8 %reduce-scatter.2.cloned.1.call-start = ((), (), s32[]{:S(2)}) async-start(), calls=%async_computation.1 | async-start | bytes 20971520 | tf_op jit(solution)/shard_map/reduce_scatter | solution.py:84
  214.9 1.6 copy-start.3
  216.5 47.4 %collective-permute-start = (bf16[1,512,2048]{2,1,0:T(8,128)(2,1)S(1)}, bf16[1,512,2048]{2,1,0:T(8,128)(2,1)}, u32[]{:S(2)}, u32[]{:S(2)}) collective-permute-start(bf16[1,512,2048]{2,1,0:T(8,128)(2,1)S(1)} %bitcast.32), channel_id=1, source_target_pairs={{0,4},{4,0},{8,12},{12,8},{1,5},{5,1},{9,13},{13,9},{2,6},{6,2},{1... | collective-permute-start | bytes 6291464 | tf_op jit(solution)/shard_map/ppermute | solution.py:24
  265.9 6.4 copy-start.5
  270.9 182.5 %collective-permute-start.1 = (bf16[2,512,2048]{2,1,0:T(8,128)(2,1)}, bf16[2,512,2048]{2,1,0:T(8,128)(2,1)}, u32[]{:S(2)}, u32[]{:S(2)}) collective-permute-start(bf16[2,512,2048]{2,1,0:T(8,128)(2,1)} %get-tuple-element.23), channel_id=1, source_target_pairs={{0,8},{4,12},{8,0},{12,4},{1,9},{5,13},{9,1},{13,5},{2,10},{6,14},... | collective-permute-start | bytes 12582920 | tf_op jit(solution)/shard_map/ppermute | solution.py:24
  272.4 181.0 %copy-start.2 = (bf16[1,2,512,2048]{3,2,1,0:T(8,128)(2,1)S(1)}, bf16[1,2,512,2048]{3,2,1,0:T(8,128)(2,1)}, u32[]{:S(2)}) copy-start(bf16[1,2,512,2048]{3,2,1,0:T(8,128)(2,1)} %get-tuple-element.22) | copy-start | bytes 12582916
  760.4 7.9 %copy-start.1 = (bf16[512,2048]{1,0:T(8,128)(2,1)S(1)}, bf16[512,2048]{1,0:T(8,128)(2,1)}, u32[]{:S(2)}) copy-start(bf16[512,2048]{1,0:T(8,128)(2,1)} %param.9) | copy-start | bytes 6291460
Sparse Core Ops, SparseCore 0:
  17.7 158.0 all-reduce.6
  189.7 287.8 all-reduce.4
  480.0 280.3 reduce-scatter.1
